TPU v7x, 32 devices: a whole 2x2x4 slice. The times are simulated.
32 devices in a mesh: row: 4 (over z), col: 8 (over y, x, core).
Axes of the slice: x: 2, y: 2, z: 4, core: 2. Of those that a mesh axis runs over, the one named last changes fastest.
Arguments:
- inverse_block: float32 [512, 512], P('row', 'col'), as said below
- panels: bfloat16 [2, 512, 512], P(None, 'row'), may hold values from -0.375 to 0.375
- pattern: int32 [2, 4], replicated, may hold values 0 or 1
Outputs:
- inverse_panel: float32 [2, 512, 512], P(None, ('row', 'col'))
- update: float32 [2, 512, 512], P(None, 'col')
Inputs may be any that keep to these rules, and one draw needn't show every extreme that they name: `pattern`: 1 marks a block of rows in the supernode's structure, 0 a block outside it. `inverse_block`: symmetric.
All inputs are finite; a program needn't handle non-finite values.
Results may differ from a plain program's by a relative error of at most 0.00045.
Values may be sent and summed in bfloat16 or wider, within the bound.
No kernel may reach another device: no remote copies, remote signals or barrier semaphores. Data moves between devices by JAX's collectives and lax.ppermute only.
A program may use at most 64 MiB of HBM per device.

v0:
```python
import jax
import jax.numpy as jnp
from jax import lax
from jax.sharding import PartitionSpec as P

BLOCK = 128


def spread(block, axis, source):
    block = jnp.where(lax.axis_index(axis) == source, block, jnp.zeros_like(block))
    return lax.psum(block, axis)


def shards(inverse_block, panels, pattern):
    row_count = lax.axis_size("row")
    col_count = lax.axis_size("col")
    row_index = lax.axis_index("row")
    col_index = lax.axis_index("col")
    rows_here = panels.shape[1]
    cols_here = inverse_block.shape[1]
    ratio = col_count // row_count
    span = rows_here // col_count
    width = panels.shape[2]
    blocks = pattern.shape[1]
    row_ids = row_index * rows_here + jnp.arange(rows_here, dtype=jnp.int32)
    onehot = (row_ids // BLOCK)[:, None] == jnp.arange(blocks, dtype=jnp.int32)[None, :]
    row_mask = jnp.sum(jnp.where(onehot[None, :, :], pattern[:, None, :], 0), axis=2)
    used = panels * row_mask[:, :, None].astype(jnp.bfloat16)
    piece = lax.dynamic_slice_in_dim(used, col_index % ratio * cols_here, cols_here, 1)
    col_panel = spread(piece, "row", col_index // ratio)
    product = jnp.einsum(
        "ij,sjw->siw", inverse_block, col_panel.astype(jnp.float32), precision=lax.Precision.HIGHEST
    )
    term = -(product * row_mask[:, :, None].astype(jnp.float32))
    share = width // col_count
    partial_update = jnp.einsum(
        "siv,siw->svw", used.astype(jnp.float32), term, precision=lax.Precision.HIGHEST
    )
    panel_parts = term.reshape(2, col_count, span, width)
    update_parts = partial_update.reshape(2, col_count, share, width)
    joined = jnp.concatenate([panel_parts, update_parts], axis=2).reshape(
        2, col_count * (span + share), width
    )
    received = lax.psum_scatter(joined, "col", scatter_dimension=1, tiled=True)
    inverse_panel = received[:, :span]
    update = -lax.psum(received[:, span:], "row")
    return (inverse_panel, update)


def solution(mesh):
    return jax.shard_map(
        shards,
        mesh=mesh,
        in_specs=(P("row", "col"), P(None, "row", None), P()),
        out_specs=(P(None, ("row", "col"), None), P(None, "col", None)),
        check_vma=False,
    )
```

profile of v0, /device:TPU:0, one launch (start us, length us, event | category | flops | bytes accessed | tf_op | source)
XLA Modules:
  0.0 142.5 jit_solution(808378041422368606)
XLA Ops:
  7.2 0.0 copy-start
  7.2 0.0 all-reduce.3.cloned.1.call-start
  7.3 0.8 select_reduce_fusion
  8.1 1.1 broadcast_multiply_fusion
  9.1 0.7 dynamic-slice_select_fusion
  9.8 0.0 all-reduce.3.cloned.1.call-update
  9.8 0.0 reduce-scatter.2.cloned.1.call-start
  9.9 38.4 %all-reduce.3.cloned.1.call-done = bf16[2,64,512]{2,1,0:T(8,128)(2,1)} async-done(((bf16[2,64,512]{2,1,0:T(8,128)(2,1)}), bf16[2,64,512]{2,1,0:T(8,128)(2,1)}) %all-reduce.3.cloned.1.call-update) | async-done | bytes 131088 | tf_op jit(solution)/shard_map/psum | solution.py:11
  48.3 0.0 copy-done
  48.3 1.3 fusion
  49.6 1.0 fusion.3
  50.7 1.7 %pad_maximum_fusion = f32[2,8,80,512]{3,2,1,0:T(8,128)} fusion(f32[2,8,64,512]{3,2,1,0:T(8,128)S(1)} %bitcast.12, f32[2,8,16,512]{3,2,1,0:T(8,128)S(1)} %bitcast.13), kind=kLoop, calls=%fused_computation | loop fusion | flops 655360 | bytes 5242880 | tf_op jit(solution)/shard_map/concatenate | solution.py:41
  52.4 0.0 reduce-scatter.2.cloned.1.call-update
  52.4 0.0 all-reduce.5.cloned.1.call-start
  52.5 43.3 %reduce-scatter.2.cloned.1.call-done = f32[2,80,512]{2,1,0:T(8,128)} async-done(((f32[2,640,512]{2,1,0:T(8,128)}), f32[2,80,512]{2,1,0:T(8,128)}) %reduce-scatter.2.cloned.1.call-update) | async-done | bytes 327696 | tf_op jit(solution)/shard_map/reduce_scatter | solution.py:44
  95.8 1.7 %slice.9 = f32[2,64,512]{2,1,0:T(8,128)} slice(f32[2,80,512]{2,1,0:T(8,128)} %reduce-scatter.2.cloned.1.call-done), slice={[0:2], [16:80], [0:512]} | slice | bytes 524288 | tf_op jit(solution)/shard_map/slice | solution.py:46
  97.4 0.0 all-reduce.5.cloned.1.call-update
  97.5 1.5 %slice.8 = f32[2,16,512]{2,1,0:T(8,128)} slice(f32[2,80,512]{2,1,0:T(8,128)} %reduce-scatter.2.cloned.1.call-done), slice={[0:2], [0:16], [0:512]} | slice | bytes 131072 | tf_op jit(solution)/shard_map/slice | solution.py:45
  98.9 35.4 %all-reduce.5.cloned.1.call-done = f32[2,64,512]{2,1,0:T(8,128)} async-done(((f32[2,64,512]{2,1,0:T(8,128)}), f32[2,64,512]{2,1,0:T(8,128)}) %all-reduce.5.cloned.1.call-update) | async-done | bytes 262160 | tf_op jit(solution)/shard_map/psum | solution.py:46
  134.3 1.7 %neg.11 = f32[2,64,512]{2,1,0:T(8,128)} negate(f32[2,64,512]{2,1,0:T(8,128)} %all-reduce.5.cloned.1.call-done) | non-fusion elementwise | flops 65536 | bytes 524288 | tf_op jit(solution)/shard_map/neg | solution.py:46
  (3 shorter events, 0.0 us)
Async XLA Ops:
  7.2 41.1 %copy-start = (f32[128,64]{0,1:T(8,128)S(1)}, f32[128,64]{0,1:T(8,128)}, u32[]{:S(2)}) copy-start(f32[128,64]{0,1:T(8,128)} %param.3) | copy-start | bytes 98308
  7.2 41.1 %all-reduce.3.cloned.1.call-start = ((), (), s32[]{:S(2)}) async-start(), calls=%async_computation.1 | async-start | bytes 262144 | tf_op jit(solution)/shard_map/psum | solution.py:11
  9.8 85.9 %reduce-scatter.2.cloned.1.call-start = ((), (), s32[]{:S(2)}) async-start(), calls=%async_computation.2 | async-start | bytes 2949120 | tf_op jit(solution)/shard_map/reduce_scatter | solution.py:44
  52.4 81.9 %all-reduce.5.cloned.1.call-start = ((), (), s32[]{:S(2)}) async-start(), calls=%async_computation.3 | async-start | bytes 524288 | tf_op jit(solution)/shard_map/psum | solution.py:46
Sparse Core Ops, SparseCore 0:
  10.9 37.3 all-reduce.2
  52.5 43.1 reduce-scatter.1
  98.7 35.5 all-reduce.4
where the time goes:
time: 143 us; the launch traced here: 142 us
  waiting for transfers between devices  117 us (82%)
  between operations  13.8 us (10%)
  other arithmetic  5.95 us (4%)
  local copies, waits for them, and re-layouts  3.16 us (2%)
  matrix products  2.35 us (2%)
    reduce_scatter x1, waiting for transfers between devices, shards(): received = lax.psum_scatter(joined, 'col', scatter_dimension=1, tiled=True)  43.3 us
    psum x1, waiting for transfers between devices, spread(): return lax.psum(block, axis)  38.4 us
    psum x1, waiting for transfers between devices, shards(): update = -lax.psum(received[:, span:], 'row')  35.4 us
  transfers between devices with their start and end apart: 3, of which 3 were waited for; matrix products, arithmetic and copies ran while one was open for 1% of the time, Pallas kernels for 0%

commit v1 on v0

--- a/solution.py
+++ b/solution.py
@@ -8,7 +8,7 @@
 
 def spread(block, axis, source):
     block = jnp.where(lax.axis_index(axis) == source, block, jnp.zeros_like(block))
-    return lax.psum(block, axis)
+    return jnp.sum(lax.all_gather(block, axis), axis=0)
 
 
 def shards(inverse_block, panels, pattern):

time: 143 us -> 123 us (0.86)
  waiting for transfers between devices: 117 us -> 80.8 us
  blocking collectives: 0 us -> 17.4 us
    psum x1 -> x0, waiting for transfers between devices: 38.4 us -> none  [spread(): return lax.psum(block, axis)]
    all_gather x0 -> x1, blocking collectives: none -> 17.4 us  [spread(): return jnp.sum(lax.all_gather(block, axis), axis=0)]
    reduce_scatter x1, waiting for transfers between devices: 43.3 us -> 45.4 us  [shards(): received = lax.psum_scatter(joined, 'col', scatter_dimension=1, tiled=True)]
  transfers between devices with their start and end apart: 3 -> 2, of which waited for: 3 -> 2; matrix products, arithmetic and copies ran while one was open for 1% -> 1% of each run, Pallas kernels for 0% -> 0%
where the time goes in v1:
time: 123 us; the launch traced here: 122 us
  waiting for transfers between devices  80.8 us (66%)
  blocking collectives  17.4 us (14%)
  between operations  14.1 us (11%)
  other arithmetic  5.37 us (4%)
  local copies, waits for them, and re-layouts  3.16 us (3%)
  matrix products  1.45 us (1%)
    reduce_scatter x1, waiting for transfers between devices, shards(): received = lax.psum_scatter(joined, 'col', scatter_dimension=1, tiled=True)  45.4 us
    psum x1, waiting for transfers between devices, shards(): update = -lax.psum(received[:, span:], 'row')  35.4 us
    all_gather x1, blocking collectives, spread(): return jnp.sum(lax.all_gather(block, axis), axis=0)  17.4 us
  transfers between devices with their start and end apart: 2, of which 2 were waited for; matrix products, arithmetic and copies ran while one was open for 1% of the time, Pallas kernels for 0%

profile of v1, /device:TPU:0, one launch (start us, length us, event | category | flops | bytes accessed | tf_op | source)
XLA Modules:
  0.0 122.3 jit_solution(11307707514112741565)
XLA Ops:
  7.2 0.0 copy-start
  7.2 0.0 reduce-scatter.2.cloned.1.call-start
  7.3 0.8 select_reduce_fusion
  8.1 1.0 broadcast_multiply_fusion
  9.2 17.4 %all-gather = bf16[8,64,512]{2,1,0:T(8,128)(2,1)S(1)} all-gather(bf16[2,64,512]{2,1,0:T(8,128)(2,1)S(1)} %dynamic-slice_select_fusion), channel_id=2, replica_groups=mesh['row'=4,'col'=8] {'row'}, dimensions={0}, use_global_device_ids=true | all-gather | bytes 655360 | tf_op jit(solution)/shard_map/all_gather | solution.py:11
  26.5 0.1 reduce_sum.22
  26.6 0.0 copy-done
  26.6 0.4 fusion
  27.0 1.0 fusion.3
  28.1 1.7 %pad_maximum_fusion = f32[2,8,80,512]{3,2,1,0:T(8,128)} fusion(f32[2,8,64,512]{3,2,1,0:T(8,128)S(1)} %bitcast.13, f32[2,8,16,512]{3,2,1,0:T(8,128)S(1)} %bitcast.14), kind=kLoop, calls=%fused_computation | loop fusion | flops 655360 | bytes 5242880 | tf_op jit(solution)/shard_map/concatenate | solution.py:41
  29.8 0.0 reduce-scatter.2.cloned.1.call-update
  29.9 0.0 all-reduce.2.cloned.1.call-start
  29.9 45.4 %reduce-scatter.2.cloned.1.call-done = f32[2,80,512]{2,1,0:T(8,128)} async-done(((f32[2,640,512]{2,1,0:T(8,128)}), f32[2,80,512]{2,1,0:T(8,128)}) %reduce-scatter.2.cloned.1.call-update) | async-done | bytes 327696 | tf_op jit(solution)/shard_map/reduce_scatter | solution.py:44
  75.3 1.7 %slice.9 = f32[2,64,512]{2,1,0:T(8,128)} slice(f32[2,80,512]{2,1,0:T(8,128)} %reduce-scatter.2.cloned.1.call-done), slice={[0:2], [16:80], [0:512]} | slice | bytes 524288 | tf_op jit(solution)/shard_map/slice | solution.py:46
  76.9 0.0 all-reduce.2.cloned.1.call-update
  77.0 1.5 %slice.8 = f32[2,16,512]{2,1,0:T(8,128)} slice(f32[2,80,512]{2,1,0:T(8,128)} %reduce-scatter.2.cloned.1.call-done), slice={[0:2], [0:16], [0:512]} | slice | bytes 131072 | tf_op jit(solution)/shard_map/slice | solution.py:45
  78.4 35.4 %all-reduce.2.cloned.1.call-done = f32[2,64,512]{2,1,0:T(8,128)} async-done(((f32[2,64,512]{2,1,0:T(8,128)}), f32[2,64,512]{2,1,0:T(8,128)}) %all-reduce.2.cloned.1.call-update) | async-done | bytes 262160 | tf_op jit(solution)/shard_map/psum | solution.py:46
  113.8 1.7 %neg.11 = f32[2,64,512]{2,1,0:T(8,128)} negate(f32[2,64,512]{2,1,0:T(8,128)} %all-reduce.2.cloned.1.call-done) | non-fusion elementwise | flops 65536 | bytes 524288 | tf_op jit(solution)/shard_map/neg | solution.py:46
  (4 shorter events, 0.1 us)
Async XLA Ops:
  7.2 19.4 %copy-start = (f32[128,64]{0,1:T(8,128)S(1)}, f32[128,64]{0,1:T(8,128)}, u32[]{:S(2)}) copy-start(f32[128,64]{0,1:T(8,128)} %param.3) | copy-start | bytes 98308
  7.2 68.1 %reduce-scatter.2.cloned.1.call-start = ((), (), s32[]{:S(2)}) async-start(), calls=%async_computation.1 | async-start | bytes 2949120 | tf_op jit(solution)/shard_map/reduce_scatter | solution.py:44
  29.9 84.0 %all-reduce.2.cloned.1.call-start = ((), (), s32[]{:S(2)}) async-start(), calls=%async_computation.2 | async-start | bytes 524288 | tf_op jit(solution)/shard_map/psum | solution.py:46
Sparse Core Ops, SparseCore 0:
  30.0 45.2 reduce-scatter.1
  78.2 35.5 all-reduce.1
